TPU v7x, 32 devices: a whole 2x2x4 slice. The times are simulated.
32 devices in a mesh: groups: 2 (over y), ctx: 16 (over z, x, core).
Axes of the slice: x: 2, y: 2, z: 4, core: 2. Of those that a mesh axis runs over, the one named last changes fastest.
Arguments:
- self_qkv: bfloat16 [3, 8192, 2048], P(None, ('groups', 'ctx')), parts along dimension 1, may hold values from -64 to 64
- windows: int32 [16], replicated, may hold values from 256 to 2048, as said below
- k_gain: float32 [2048], replicated, may hold values from 0.25 to 1.75
- cont_qkv: bfloat16 [3, 256, 2048], P(None, ('groups', 'ctx')), parts along dimension 1, may hold values from -64 to 64
- starts: int32 [32], P('groups'), parts along dimension 0, may hold values from 1 to 4096
Outputs:
- self_out: bfloat16 [8192, 2048], P(('groups', 'ctx')), parts along dimension 0
- cross_out: bfloat16 [256, 2048], P(('groups', 'ctx')), parts along dimension 0
There are 2 independent parts, one for each index of `groups`. A program takes and returns all parts, laid end to end along the dimension named above; an argument that names none is the same for every part. Nothing has to cross between parts.
Inputs may be any that keep to these rules, and one draw needn't show every extreme that they name: `windows`: some head has a window of exactly 2048.
All inputs are finite; a program needn't handle non-finite values.
Results may differ from a plain program's by a relative error of at most 0.0055.
Values may be sent and summed in bfloat16 or wider, within the bound.
No kernel may reach another device: no remote copies, remote signals or barrier semaphores. Data moves between devices by JAX's collectives and lax.ppermute only.
A program may use at most 128 MiB of HBM per device.

v0:
```python
import math
import jax
import jax.numpy as jnp
from jax import lax
from jax.sharding import PartitionSpec as P

WIN = 2048
CLEN = 8
EPSILON = 1e-06
NEGATIVE = -1e30


def shifted(value, axis, steps):
    count = lax.axis_size(axis)
    initial, last = (max(0, -steps), min(count, count - steps))
    return lax.ppermute(value, axis, [(source, source + steps) for source in range(initial, last)])


def finish_rows(cache_high, cache_totals, weighted, own_rows):
    rows_here = own_rows.shape[1]
    features = own_rows.shape[2]
    head_count = cache_high.shape[1]
    head_dim = features // head_count
    groups_here = rows_here // CLEN
    parts = own_rows.reshape(3, groups_here, CLEN, head_count, head_dim)
    scaling = 1.0 / math.sqrt(head_dim)
    scores = (
        jnp.einsum("cihd,cjhd->hcij", parts[0], parts[1], preferred_element_type=jnp.float32)
        * scaling
    )
    causal = (jnp.arange(CLEN)[None, :] <= jnp.arange(CLEN)[:, None])[None, None]
    scores = jnp.where(causal, scores, NEGATIVE)
    prior_high = cache_high.T.reshape(head_count, groups_here, CLEN)
    final = jnp.maximum(prior_high, jnp.max(scores, axis=-1))
    rescale = jnp.exp(prior_high - final)
    expo = jnp.where(causal, jnp.exp(scores - final[..., None]), 0.0)
    totals = rescale * cache_totals.T.reshape(head_count, groups_here, CLEN) + jnp.sum(
        expo, axis=-1
    )
    own_sum = jnp.einsum(
        "hcij,cjhd->cihd", expo.astype(jnp.bfloat16), parts[2], preferred_element_type=jnp.float32
    )
    merged = (
        weighted.reshape(groups_here, CLEN, head_count, head_dim)
        * jnp.transpose(rescale, (1, 2, 0))[..., None]
        + own_sum
    )
    result = merged / jnp.transpose(totals, (1, 2, 0))[..., None]
    return result.reshape(rows_here, features).astype(jnp.bfloat16)


def per_device(self_qkv, windows, k_gain, cont_qkv, starts):
    length = self_qkv.shape[1]
    features = self_qkv.shape[2]
    head_count = windows.shape[0]
    head_dim = features // head_count
    scaling = 1.0 / math.sqrt(head_dim)
    anchor = lax.axis_index("ctx") * length
    reach = WIN // length
    width = (reach + 1) * length
    key_value = self_qkv[1:3]
    earlier = []
    for distance in range(1, reach + 1):
        earlier.append(shifted(key_value, "ctx", distance))
    band = jnp.concatenate(earlier[::-1] + [key_value], axis=1)
    distance_grid = (
        jnp.arange(length, dtype=jnp.int32)[:, None]
        + reach * length
        - jnp.arange(width, dtype=jnp.int32)[None, :]
    )
    key_position = anchor - reach * length + jnp.arange(width, dtype=jnp.int32)

    def one_head(head):
        offset = head * head_dim
        queries = lax.dynamic_slice_in_dim(self_qkv[0], offset, head_dim, 1)
        keys = lax.dynamic_slice_in_dim(band[0], offset, head_dim, 1)
        values = lax.dynamic_slice_in_dim(band[1], offset, head_dim, 1)
        scores = (
            jnp.einsum("id,jd->ij", queries, keys, preferred_element_type=jnp.float32) * scaling
        )
        visible = (
            (distance_grid >= 0) & (distance_grid < windows[head]) & (key_position >= 0)[None, :]
        )
        scores = jnp.where(visible, scores, NEGATIVE)
        highest = jnp.max(scores, axis=-1, keepdims=True)
        expo = jnp.where(visible, jnp.exp(scores - highest), 0.0)
        weights = (expo / jnp.sum(expo, axis=-1, keepdims=True)).astype(jnp.bfloat16)
        return jnp.dot(weights, values, preferred_element_type=jnp.float32).astype(jnp.bfloat16)

    attended = lax.map(one_head, jnp.arange(head_count, dtype=jnp.int32))
    self_out = jnp.transpose(attended, (1, 0, 2)).reshape(length, features)
    hidden = self_out.astype(jnp.float32).reshape(length, head_count, head_dim)
    normed = hidden * lax.rsqrt(jnp.mean(hidden * hidden, axis=-1, keepdims=True) + EPSILON)
    cache_keys = (
        (normed.reshape(length, features) * k_gain)
        .astype(jnp.bfloat16)
        .reshape(length, head_count, head_dim)
    )
    cache_values = self_out.reshape(length, head_count, head_dim)
    gathered = lax.all_gather(cont_qkv[0], "ctx", axis=0, tiled=True)
    rows_all = gathered.shape[0]
    rows_here = cont_qkv.shape[1]
    conts_all = starts.shape[0]
    row_start = jnp.broadcast_to(starts[:, None], (conts_all, rows_all // conts_all)).reshape(
        rows_all
    )
    positions = anchor + jnp.arange(length, dtype=jnp.int32)
    block = math.gcd(rows_all, 512)
    block_count = rows_all // block
    query_blocks = gathered.reshape(block_count, block, head_count, head_dim)
    start_blocks = row_start.reshape(block_count, block)

    def block_scores(query_block, start_block):
        raw = (
            jnp.einsum("ihd,jhd->hij", query_block, cache_keys, preferred_element_type=jnp.float32)
            * scaling
        )
        seen = (positions[None, :] < start_block[:, None])[None]
        return (jnp.where(seen, raw, NEGATIVE), seen)

    def local_part(inputs):
        query_block, start_block = inputs
        masked, seen = block_scores(query_block, start_block)
        peak = jnp.max(masked, axis=-1)
        local_expo = jnp.where(seen, jnp.exp(masked - peak[..., None]), 0.0)
        totals = jnp.sum(local_expo, axis=-1)
        summed = jnp.einsum(
            "hij,jhd->ihd",
            local_expo.astype(jnp.bfloat16),
            cache_values,
            preferred_element_type=jnp.float32,
        )
        return (summed.reshape(block, features), peak.T, totals.T)

    summed, peaks, totals = lax.map(local_part, (query_blocks, start_blocks))
    sources = lax.axis_size("ctx")
    summed = summed.reshape(sources, rows_here, features)
    peaks = peaks.reshape(sources, rows_here, head_count)
    totals = totals.reshape(sources, rows_here, head_count)
    summed_in, peaks_in, totals_in = (
        lax.all_to_all(
            summed.astype(jnp.bfloat16), "ctx", split_axis=0, concat_axis=0, tiled=True
        ).astype(summed.dtype),
        lax.all_to_all(
            peaks.astype(jnp.bfloat16), "ctx", split_axis=0, concat_axis=0, tiled=True
        ).astype(peaks.dtype),
        lax.all_to_all(
            totals.astype(jnp.bfloat16), "ctx", split_axis=0, concat_axis=0, tiled=True
        ).astype(totals.dtype),
    )
    cache_high = jnp.max(peaks_in, axis=0)
    rescale = jnp.exp(peaks_in - cache_high[None])
    weighted = jnp.sum(
        summed_in.reshape(sources, rows_here, head_count, head_dim) * rescale[..., None], axis=0
    )
    cache_totals = jnp.sum(rescale * totals_in, axis=0)
    cross_out = finish_rows(cache_high, cache_totals, weighted, cont_qkv)
    return (self_out, cross_out)


def solution(mesh):
    in_specs = (
        P(None, ("groups", "ctx"), None),
        P(),
        P(),
        P(None, ("groups", "ctx"), None),
        P("groups"),
    )
    out_specs = (P(("groups", "ctx"), None), P(("groups", "ctx"), None))
    return jax.shard_map(
        per_device, mesh=mesh, in_specs=in_specs, out_specs=out_specs, check_vma=False
    )
```

profile of v0, /device:TPU:0, one launch (start us, length us, event | category | flops | bytes accessed | tf_op | source)
XLA Modules:
  0.0 854.6 jit_solution(9346026822741052805)
XLA Ops:
  0.7 3.2 slice.25
  3.9 7.3 collective-permute-start
  11.2 4.9 collective-permute-start.1
  16.1 3.5 collective-permute-start.2
  23.8 32.4 %collective-permute-done = bf16[2,256,2048]{2,1,0:T(8,128)(2,1)} collective-permute-done((bf16[2,256,2048]{2,1,0:T(8,128)(2,1)}, bf16[2,256,2048]{2,1,0:T(8,128)(2,1)}, u32[]{:S(2)}, u32[]{:S(2)}) %collective-permute-start) | collective-permute-done | bytes 2097184 | tf_op jit(solution)/shard_map/ppermute | solution.py:16
  59.1 301.0 %all-gather = bf16[1,128,2048]{2,1,0:T(8,128)(2,1)S(1)} all-gather(bf16[1,8,2048]{2,1,0:T(8,128)(2,1)S(1)} %slice-done), channel_id=2, replica_groups=mesh['groups'=2,'ctx'=16] {'ctx'}, dimensions={1}, use_global_device_ids=true | all-gather | bytes 557056 | tf_op jit(solution)/shard_map/all_gather | solution.py:100
  360.0 3.6 collective-permute-start.6
  376.9 30.9 %collective-permute-done.6 = bf16[2,256,2048]{2,1,0:T(8,128)(2,1)} collective-permute-done((bf16[2,256,2048]{2,1,0:T(8,128)(2,1)}, bf16[2,256,2048]{2,1,0:T(8,128)(2,1)}, u32[]{:S(2)}, u32[]{:S(2)}) %collective-permute-start.6) | collective-permute-done | bytes 2097184 | tf_op jit(solution)/shard_map/ppermute | solution.py:16
  412.3 6.5 copy-done
  418.7 278.3 %while.8 = (s32[]{:T(128)}, bf16[16,256,128]{2,1,0:T(8,128)(2,1)}, s32[16]{0:T(128)S(1)}, s32[16]{0:T(128)S(1)}, bf16[3,256,2048]{2,1,0:T(8,128)(2,1)S(1)}, /*in...) while((s32[]{:T(128)}, bf16[16,256,128]{2,1,0:T(8,128)(2,1)}, ...), condition=%wide.region_3.4_spmd.clone.clone, body=%wide.region_0.3_spmd.clone.clone.sunk | while | flops 316772352 | bytes 48255728 | solution.py:90
  422.0 8.1 fusion.75
  439.4 8.1 fusion.75
  456.8 8.1 fusion.75
  474.2 8.1 fusion.75
  491.6 8.1 fusion.75
  509.0 8.1 fusion.75
  526.4 8.1 fusion.75
  543.8 8.1 fusion.75
  561.2 8.1 fusion.75
  578.6 8.1 fusion.75
  595.9 8.1 fusion.75
  613.3 8.1 fusion.75
  630.8 8.1 fusion.75
  648.1 8.1 fusion.75
  665.5 8.1 fusion.75
  682.9 8.1 fusion.75
  702.3 116.6 %all-to-all-start.2 = ((bf16[16,8,16]{2,1,0:T(8,128)(2,1)}), bf16[16,8,16]{2,1,0:T(8,128)(2,1)S(1)}, u32[]{:S(2)}, u32[]{:S(2)}) async-start(bf16[16,8,16]{2,1,0:T(8,128)(2,1)} %bitcast.20), calls=%async_computation.2 | async-start | bytes 65536 | tf_op jit(solution)/shard_map/all_to_all | solution.py:147
  819.7 5.9 all-to-all-done.2
  825.6 3.5 all-to-all-start.1
  832.6 3.1 all-to-all-done.1
  835.7 3.6 all-to-all-start
  842.2 11.3 %all-to-all-done = bf16[16,8,2048]{2,1,0:T(8,128)(2,1)S(1)} async-done(((bf16[16,8,2048]{2,1,0:T(8,128)(2,1)}), bf16[16,8,2048]{2,1,0:T(8,128)(2,1)S(1)}, u32[]{:S(2)}, u32[]{:S(2)}) %all-to-all-start) | async-done | bytes 524320 | tf_op jit(solution)/shard_map/all_to_all | solution.py:141
  (179 shorter events, 151.1 us)
Async XLA Ops:
  0.6 23.0 %copy-start.2 = (bf16[3,8,2048]{2,1,0:T(8,128)(2,1)S(1)}, bf16[3,8,2048]{2,1,0:T(8,128)(2,1)}, u32[]{:S(2)}) copy-start(bf16[3,8,2048]{2,1,0:T(8,128)(2,1)} %param.10) | copy-start | bytes 294916
  0.6 58.4 %slice-start = ((bf16[3,8,2048]{2,1,0:T(8,128)(2,1)}), bf16[1,8,2048]{2,1,0:T(8,128)(2,1)S(1)}, s32[]{:S(2)}) async-start(bf16[3,8,2048]{2,1,0:T(8,128)(2,1)} %param.10), calls=%async_computation.3 | async-start | bytes 65536 | tf_op jit(solution)/shard_map/slice | solution.py:100
  0.7 58.2 %copy-start.3 = (s32[16]{0:T(128)S(1)}, s32[16]{0:T(128)}, u32[]{:S(2)}) copy-start(s32[16]{0:T(128)} %param.11) | copy-start | bytes 196
  3.9 52.3 %collective-permute-start = (bf16[2,256,2048]{2,1,0:T(8,128)(2,1)}, bf16[2,256,2048]{2,1,0:T(8,128)(2,1)}, u32[]{:S(2)}, u32[]{:S(2)}) collective-permute-start(bf16[2,256,2048]{2,1,0:T(8,128)(2,1)} %slice.25), channel_id=1, source_target_pairs={{0,8},{1,9},{2,10},{3,11},{4,12},{5,13},{6,14},{7,15},{16,24},{17,... | collective-permute-start | bytes 6291464 | tf_op jit(solution)/shard_map/ppermute | solution.py:16
  11.2 348.9 %collective-permute-start.1 = (bf16[2,256,2048]{2,1,0:T(8,128)(2,1)}, bf16[2,256,2048]{2,1,0:T(8,128)(2,1)}, u32[]{:S(2)}, u32[]{:S(2)}) collective-permute-start(bf16[2,256,2048]{2,1,0:T(8,128)(2,1)} %slice.25), channel_id=1, source_target_pairs={{0,7},{1,8},{2,9},{3,10},{4,11},{5,12},{6,13},{7,14},{8,15},{16,23... | collective-permute-start | bytes 6291464 | tf_op jit(solution)/shard_map/ppermute | solution.py:16
  16.1 347.7 %collective-permute-start.2 = (bf16[2,256,2048]{2,1,0:T(8,128)(2,1)}, bf16[2,256,2048]{2,1,0:T(8,128)(2,1)}, u32[]{:S(2)}, u32[]{:S(2)}) collective-permute-start(bf16[2,256,2048]{2,1,0:T(8,128)(2,1)} %slice.25), channel_id=1, source_target_pairs={{0,6},{1,7},{2,8},{3,9},{4,10},{5,11},{6,12},{7,13},{8,14},{9,15},... | collective-permute-start | bytes 6291464 | tf_op jit(solution)/shard_map/ppermute | solution.py:16
  19.6 353.7 %collective-permute-start.3 = (bf16[2,256,2048]{2,1,0:T(8,128)(2,1)}, bf16[2,256,2048]{2,1,0:T(8,128)(2,1)}, u32[]{:S(2)}, u32[]{:S(2)}) collective-permute-start(bf16[2,256,2048]{2,1,0:T(8,128)(2,1)} %slice.25), channel_id=1, source_target_pairs={{0,5},{1,6},{2,7},{3,8},{4,9},{5,10},{6,11},{7,12},{8,13},{9,14},{... | collective-permute-start | bytes 6291464 | tf_op jit(solution)/shard_map/ppermute | solution.py:16
  22.2 352.8 %collective-permute-start.4 = (bf16[2,256,2048]{2,1,0:T(8,128)(2,1)}, bf16[2,256,2048]{2,1,0:T(8,128)(2,1)S(1)}, u32[]{:S(2)}, u32[]{:S(2)}) collective-permute-start(bf16[2,256,2048]{2,1,0:T(8,128)(2,1)} %slice.25), channel_id=1, source_target_pairs={{0,4},{1,5},{2,6},{3,7},{4,8},{5,9},{6,10},{7,11},{8,12},{9,13},{1... | collective-permute-start | bytes 6291464 | tf_op jit(solution)/shard_map/ppermute | solution.py:16
  56.2 319.0 %collective-permute-start.5 = (bf16[2,256,2048]{2,1,0:T(8,128)(2,1)}, bf16[2,256,2048]{2,1,0:T(8,128)(2,1)}, u32[]{:S(2)}, u32[]{:S(2)}) collective-permute-start(bf16[2,256,2048]{2,1,0:T(8,128)(2,1)} %slice.25), channel_id=1, source_target_pairs={{0,3},{1,4},{2,5},{3,6},{4,7},{5,8},{6,9},{7,10},{8,11},{9,12},{10... | collective-permute-start | bytes 6291464 | tf_op jit(solution)/shard_map/ppermute | solution.py:16
  360.0 47.8 %collective-permute-start.6 = (bf16[2,256,2048]{2,1,0:T(8,128)(2,1)}, bf16[2,256,2048]{2,1,0:T(8,128)(2,1)}, u32[]{:S(2)}, u32[]{:S(2)}) collective-permute-start(bf16[2,256,2048]{2,1,0:T(8,128)(2,1)} %slice.25), channel_id=1, source_target_pairs={{0,2},{1,3},{2,4},{3,5},{4,6},{5,7},{6,8},{7,9},{8,10},{9,11},{10,... | collective-permute-start | bytes 6291464 | tf_op jit(solution)/shard_map/ppermute | solution.py:16
  363.8 45.8 %collective-permute-start.7 = (bf16[2,256,2048]{2,1,0:T(8,128)(2,1)}, bf16[2,256,2048]{2,1,0:T(8,128)(2,1)}, u32[]{:S(2)}, u32[]{:S(2)}) collective-permute-start(bf16[2,256,2048]{2,1,0:T(8,128)(2,1)} %slice.25), channel_id=1, source_target_pairs={{0,1},{1,2},{2,3},{3,4},{4,5},{5,6},{6,7},{7,8},{8,9},{9,10},{10,1... | collective-permute-start | bytes 6291464 | tf_op jit(solution)/shard_map/ppermute | solution.py:16
  409.6 2.5 copy-start.1
  412.1 6.6 copy-start.5
  412.3 6.5 copy-start
  418.7 280.1 %copy-start.4 = (f32[2048]{0:T(1024)S(1)}, f32[2048]{0:T(1024)}, u32[]{:S(2)}) copy-start(f32[2048]{0:T(1024)} %param.9) | copy-start | bytes 24580
  702.3 123.3 %all-to-all-start.2 = ((bf16[16,8,16]{2,1,0:T(8,128)(2,1)}), bf16[16,8,16]{2,1,0:T(8,128)(2,1)S(1)}, u32[]{:S(2)}, u32[]{:S(2)}) async-start(bf16[16,8,16]{2,1,0:T(8,128)(2,1)} %bitcast.20), calls=%async_computation.2 | async-start | bytes 65536 | tf_op jit(solution)/shard_map/all_to_all | solution.py:147
  825.6 10.1 %all-to-all-start.1 = ((bf16[16,8,16]{2,1,0:T(8,128)(2,1)}), bf16[16,8,16]{2,1,0:T(8,128)(2,1)S(1)}, u32[]{:S(2)}, u32[]{:S(2)}) async-start(bf16[16,8,16]{2,1,0:T(8,128)(2,1)} %bitcast.6), calls=%async_computation.1 | async-start | bytes 65536 | tf_op jit(solution)/shard_map/all_to_all | solution.py:144
  835.7 17.8 %all-to-all-start = ((bf16[16,8,2048]{2,1,0:T(8,128)(2,1)}), bf16[16,8,2048]{2,1,0:T(8,128)(2,1)S(1)}, u32[]{:S(2)}, u32[]{:S(2)}) async-start(bf16[16,8,2048]{2,1,0:T(8,128)(2,1)} %convert_element_type.69), calls=%async_computation | async-start | bytes 1048576 | tf_op jit(solution)/shard_map/all_to_all | solution.py:141
where the time goes:
time: 856 us; the launch traced here: 855 us
  blocking collectives  301 us (35%)
  local copies, waits for them, and re-layouts  179 us (21%)
  starting transfers between devices  153 us (18%)
  waiting for transfers between devices  83.7 us (10%)
  matrix products  71.8 us (8%)
  loops' own time  35.4 us (4%)
  other arithmetic  30.3 us (4%)
    all_gather x1, blocking collectives, per_device(): gathered = lax.all_gather(cont_qkv[0], 'ctx', axis=0, tiled=True)  301 us
    slice x16, local copies, waits for them, and re-layouts, one_head(): values = lax.dynamic_slice_in_dim(band[1], offset, head_dim, 1)  130 us
    all_to_all x1, starting transfers between devices, per_device(): lax.all_to_all(totals.astype(jnp.bfloat16), 'ctx', split_axis=0, concat_a...  117 us
    ppermute x8, waiting for transfers between devices, shifted(): lax.ppermute(value, axis, [(source, source + steps) for source in range(i...  63.4 us
    dot_general x16, matrix products, one_head(): jnp.dot(weights, values, preferred_element_type=jnp.float32)  39.7 us
    another operation x1, loops' own time, per_device(): attended = lax.map(one_head, jnp.arange(head_count, dtype=jnp.int32))  35.4 us
    ppermute x8, starting transfers between devices, shifted(): lax.ppermute(value, axis, [(source, source + steps) for source in range(i...  29.1 us
    reduce_sum x16, other arithmetic, one_head(): jnp.sum(expo, axis=-1, keepdims=True)  27.1 us
  transfers between devices with their start and end apart: 11, of which 5 were waited for; matrix products, arithmetic and copies ran while one was open for 2% of the time, Pallas kernels for 0%

commit v1 on v0

--- a/solution.py
+++ b/solution.py
@@ -97,7 +97,12 @@
         .reshape(length, head_count, head_dim)
     )
     cache_values = self_out.reshape(length, head_count, head_dim)
-    gathered = lax.all_gather(cont_qkv[0], "ctx", axis=0, tiled=True)
+    ring = [cont_qkv[0]]
+    for hop in range(15):
+        ring.append(lax.ppermute(ring[-1], "ctx", [(dev, (dev + 1) % 16) for dev in range(16)]))
+    gathered = jnp.roll(
+        jnp.concatenate(ring[::-1], axis=0), (lax.axis_index("ctx") + 1) * ring[0].shape[0], axis=0
+    )
     rows_all = gathered.shape[0]
     rows_here = cont_qkv.shape[1]
     conts_all = starts.shape[0]

time: 856 us -> 982 us (1.15)
  blocking collectives: 301 us -> 0 us
  starting transfers between devices: 153 us -> 454 us
  waiting for transfers between devices: 83.7 us -> 182 us
  local copies, waits for them, and re-layouts: 179 us -> 204 us
    all_gather x1 -> x0, blocking collectives: 301 us -> none  [per_device(): gathered = lax.all_gather(cont_qkv[0], 'ctx', axis=0, tiled=True)]
    ppermute x0 -> x15, starting transfers between devices: none -> 282 us  [per_device(): lax.ppermute(ring[-1], 'ctx', [(dev, (dev + 1) % 16) for dev in range(16)])]
    ppermute x0 -> x15, waiting for transfers between devices: none -> 109 us  [per_device(): lax.ppermute(ring[-1], 'ctx', [(dev, (dev + 1) % 16) for dev in range(16)])]
    ppermute x8, starting transfers between devices: 29.1 us -> 103 us  [shifted(): lax.ppermute(value, axis, [(source, source + steps) for source in range(i...]
    all_to_all x1, starting transfers between devices: 117 us -> 60.7 us  [per_device(): lax.all_to_all(totals.astype(jnp.bfloat16), 'ctx', split_axis=0, concat_a...]
    concatenate x0 -> x1, local copies, waits for them, and re-layouts: none -> 15.6 us  [per_device(): jnp.roll(jnp.concatenate(ring[::-1], axis=0), (lax.axis_index('ctx') + 1)...]
    ppermute x8, waiting for transfers between devices: 63.4 us -> 52.9 us  [shifted(): lax.ppermute(value, axis, [(source, source + steps) for source in range(i...]
    unnamed x20 -> x45, local copies, waits for them, and re-layouts: 19.5 us -> 28.7 us
  transfers between devices with their start and end apart: 11 -> 26, of which waited for: 5 -> 19; matrix products, arithmetic and copies ran while one was open for 2% -> 4% of each run, Pallas kernels for 0% -> 0%
where the time goes in v1:
time: 982 us; the launch traced here: 979 us
  starting transfers between devices  454 us (46%)
  local copies, waits for them, and re-layouts  204 us (21%)
  waiting for transfers between devices  182 us (19%)
  matrix products  72.7 us (7%)
  loops' own time  35.4 us (4%)
  other arithmetic  30.6 us (3%)
    ppermute x15, starting transfers between devices, per_device(): lax.ppermute(ring[-1], 'ctx', [(dev, (dev + 1) % 16) for dev in range(16)])  282 us
    slice x16, local copies, waits for them, and re-layouts, one_head(): values = lax.dynamic_slice_in_dim(band[1], offset, head_dim, 1)  130 us
    ppermute x15, waiting for transfers between devices, per_device(): lax.ppermute(ring[-1], 'ctx', [(dev, (dev + 1) % 16) for dev in range(16)])  109 us
    ppermute x8, starting transfers between devices, shifted(): lax.ppermute(value, axis, [(source, source + steps) for source in range(i...  103 us
    all_to_all x1, starting transfers between devices, per_device(): lax.all_to_all(totals.astype(jnp.bfloat16), 'ctx', split_axis=0, concat_a...  60.7 us
    ppermute x8, waiting for transfers between devices, shifted(): lax.ppermute(value, axis, [(source, source + steps) for source in range(i...  52.9 us
    dot_general x16, matrix products, one_head(): jnp.dot(weights, values, preferred_element_type=jnp.float32)  39.8 us
    another operation x1, loops' own time, per_device(): attended = lax.map(one_head, jnp.arange(head_count, dtype=jnp.int32))  35.4 us
  transfers between devices with their start and end apart: 26, of which 19 were waited for; matrix products, arithmetic and copies ran while one was open for 4% of the time, Pallas kernels for 0%

profile of v1, /device:TPU:0, one launch (start us, length us, event | category | flops | bytes accessed | tf_op | source)
XLA Modules:
  0.0 978.9 jit_solution(16049359270139672326)
XLA Ops:
  19.9 11.3 %collective-permute-done.8 = bf16[8,2048]{0,1:T(8,128)(2,1)S(1)} collective-permute-done((bf16[8,2048]{0,1:T(8,128)(2,1)S(1)}, bf16[8,2048]{0,1:T(8,128)(2,1)S(1)}, u32[]{:S(2)}, u32[]{:S(2)}) %collective-permute-start.8) | collective-permute-done | bytes 32800 | tf_op jit(solution)/shard_map/ppermute | solution.py:102
  31.2 11.3 %collective-permute-done.9 = bf16[8,2048]{0,1:T(8,128)(2,1)S(1)} collective-permute-done((bf16[8,2048]{0,1:T(8,128)(2,1)S(1)}, bf16[8,2048]{0,1:T(8,128)(2,1)S(1)}, u32[]{:S(2)}, u32[]{:S(2)}) %collective-permute-start.9) | collective-permute-done | bytes 32800 | tf_op jit(solution)/shard_map/ppermute | solution.py:102
  42.5 38.2 %collective-permute-done.10 = bf16[8,2048]{0,1:T(8,128)(2,1)S(1)} collective-permute-done((bf16[8,2048]{0,1:T(8,128)(2,1)S(1)}, bf16[8,2048]{0,1:T(8,128)(2,1)S(1)}, u32[]{:S(2)}, u32[]{:S(2)}) %collective-permute-start.10) | collective-permute-done | bytes 32800 | tf_op jit(solution)/shard_map/ppermute | solution.py:102
  80.8 79.1 %collective-permute-start.11 = (bf16[8,2048]{0,1:T(8,128)(2,1)S(1)}, bf16[8,2048]{0,1:T(8,128)(2,1)S(1)}, u32[]{:S(2)}, u32[]{:S(2)}) collective-permute-start(bf16[8,2048]{0,1:T(8,128)(2,1)S(1)} %collective-permute-done.10), channel_id=1, source_target_pairs={{0,1},{1,2},{2,3},{3,4},{4,5},{5,6},{6,7},{7,8},{8,9},{9,10},{10,1... | collective-permute-start | bytes 98312 | tf_op jit(solution)/shard_map/ppermute | solution.py:102
  198.5 117.8 %collective-permute-start.15 = (bf16[8,2048]{0,1:T(8,128)(2,1)S(1)}, bf16[8,2048]{0,1:T(8,128)(2,1)S(1)}, u32[]{:S(2)}, u32[]{:S(2)}) collective-permute-start(bf16[8,2048]{0,1:T(8,128)(2,1)S(1)} %collective-permute-done.14), channel_id=1, source_target_pairs={{0,1},{1,2},{2,3},{3,4},{4,5},{5,6},{6,7},{7,8},{8,9},{9,10},{10,1... | collective-permute-start | bytes 98312 | tf_op jit(solution)/shard_map/ppermute | solution.py:102
  318.7 8.0 collective-permute-start.16
  347.2 27.3 %collective-permute-start.3 = (bf16[2,256,2048]{2,1,0:T(8,128)(2,1)}, bf16[2,256,2048]{2,1,0:T(8,128)(2,1)}, u32[]{:S(2)}, u32[]{:S(2)}) collective-permute-start(bf16[2,256,2048]{2,1,0:T(8,128)(2,1)} %slice.25), channel_id=1, source_target_pairs={{0,5},{1,6},{2,7},{3,8},{4,9},{5,10},{6,11},{7,12},{8,13},{9,14},{... | collective-permute-start | bytes 6291464 | tf_op jit(solution)/shard_map/ppermute | solution.py:16
  410.8 34.0 %collective-permute-start.22 = (bf16[8,2048]{0,1:T(8,128)(2,1)S(1)}, bf16[8,2048]{0,1:T(8,128)(2,1)S(1)}, u32[]{:S(2)}, u32[]{:S(2)}) collective-permute-start(bf16[8,2048]{0,1:T(8,128)(2,1)S(1)} %collective-permute-done.21), channel_id=1, source_target_pairs={{0,1},{1,2},{2,3},{3,4},{4,5},{5,6},{6,7},{7,8},{8,9},{9,10},{10,1... | collective-permute-start | bytes 98312 | tf_op jit(solution)/shard_map/ppermute | solution.py:102
  446.4 29.2 %collective-permute-start.4 = (bf16[2,256,2048]{2,1,0:T(8,128)(2,1)}, bf16[2,256,2048]{2,1,0:T(8,128)(2,1)}, u32[]{:S(2)}, u32[]{:S(2)}) collective-permute-start(bf16[2,256,2048]{2,1,0:T(8,128)(2,1)} %slice.25), channel_id=1, source_target_pairs={{0,4},{1,5},{2,6},{3,7},{4,8},{5,9},{6,10},{7,11},{8,12},{9,13},{1... | collective-permute-start | bytes 6291464 | tf_op jit(solution)/shard_map/ppermute | solution.py:16
  475.7 25.3 %collective-permute-start.5 = (bf16[2,256,2048]{2,1,0:T(8,128)(2,1)}, bf16[2,256,2048]{2,1,0:T(8,128)(2,1)}, u32[]{:S(2)}, u32[]{:S(2)}) collective-permute-start(bf16[2,256,2048]{2,1,0:T(8,128)(2,1)} %slice.25), channel_id=1, source_target_pairs={{0,3},{1,4},{2,5},{3,6},{4,7},{5,8},{6,9},{7,10},{8,11},{9,12},{10... | collective-permute-start | bytes 6291464 | tf_op jit(solution)/shard_map/ppermute | solution.py:16
  504.1 15.6 %concatenate.10 = bf16[256,2048]{0,1:T(8,128)(2,1)S(1)} concatenate(bf16[8,2048]{0,1:T(8,128)(2,1)} %copy-done.13, bf16[8,2048]{0,1:T(8,128)(2,1)} %copy-done.12, bf16[8,2048]{0,1:T(8,128)(2,1)} %copy-done.11, bf16[8,2048]{0,1:T(8,128)(2,1)} %copy-done.10, bf16[8,2048]{0,1:T(8,128)(2,1)} %copy-done.9, bf16[8,2048]{0,1:T(8,128)(2,1)} %copy-done.8, bf16[8,2048]{0,1:T(8,128)(2,1)} %copy-done.7, ...), dimensions={0} | concatenate | bytes 2097152 | tf_op jit(solution)/shard_map/jit(_roll_dynamic)/concatenate | solution.py:103
  532.7 9.7 collective-permute-done.5
  544.2 43.2 %collective-permute-done.6 = bf16[2,256,2048]{2,1,0:T(8,128)(2,1)} collective-permute-done((bf16[2,256,2048]{2,1,0:T(8,128)(2,1)}, bf16[2,256,2048]{2,1,0:T(8,128)(2,1)}, u32[]{:S(2)}, u32[]{:S(2)}) %collective-permute-start.6) | collective-permute-done | bytes 2097184 | tf_op jit(solution)/shard_map/ppermute | solution.py:16
  597.6 278.4 %while.8 = (s32[]{:T(128)}, bf16[16,256,128]{2,1,0:T(8,128)(2,1)}, s32[16]{0:T(128)S(1)}, s32[16]{0:T(128)S(1)}, bf16[3,256,2048]{2,1,0:T(8,128)(2,1)S(1)}, /*in...) while((s32[]{:T(128)}, bf16[16,256,128]{2,1,0:T(8,128)(2,1)}, ...), condition=%wide.region_3.4_spmd.clone.clone, body=%wide.region_0.3_spmd.clone.clone.sunk | while | flops 316772352 | bytes 48255728 | solution.py:90
  600.9 8.1 fusion.75
  618.3 8.1 fusion.75
  635.7 8.1 fusion.75
  653.1 8.1 fusion.75
  670.5 8.1 fusion.75
  687.9 8.1 fusion.75
  705.3 8.1 fusion.75
  722.7 8.1 fusion.75
  740.1 8.1 fusion.75
  757.5 8.1 fusion.75
  774.9 8.1 fusion.75
  792.3 8.1 fusion.75
  809.7 8.1 fusion.75
  827.1 8.1 fusion.75
  844.5 8.1 fusion.75
  861.9 8.1 fusion.75
  882.5 60.7 %all-to-all-start.2 = ((bf16[16,8,16]{2,1,0:T(8,128)(2,1)}), bf16[16,8,16]{2,1,0:T(8,128)(2,1)S(1)}, u32[]{:S(2)}, u32[]{:S(2)}) async-start(bf16[16,8,16]{2,1,0:T(8,128)(2,1)} %bitcast.20), calls=%async_computation.2 | async-start | bytes 65536 | tf_op jit(solution)/shard_map/all_to_all | solution.py:152
  966.4 11.3 %all-to-all-done = bf16[16,8,2048]{2,1,0:T(8,128)(2,1)S(1)} async-done(((bf16[16,8,2048]{2,1,0:T(8,128)(2,1)}), bf16[16,8,2048]{2,1,0:T(8,128)(2,1)S(1)}, u32[]{:S(2)}, u32[]{:S(2)}) %all-to-all-start) | async-done | bytes 524320 | tf_op jit(solution)/shard_map/all_to_all | solution.py:146
  (234 shorter events, 290.8 us)
Async XLA Ops:
  0.6 19.0 %slice-start = ((bf16[3,8,2048]{2,1,0:T(8,128)(2,1)}), bf16[1,8,2048]{2,1,0:T(8,128)(2,1)S(1)}, s32[]{:S(2)}) async-start(bf16[3,8,2048]{2,1,0:T(8,128)(2,1)} %param.10), calls=%async_computation.3 | async-start | bytes 65536 | tf_op jit(solution)/shard_map/slice | solution.py:100
  0.6 475.0 %copy-start.14 = (bf16[3,8,2048]{2,1,0:T(8,128)(2,1)S(1)}, bf16[3,8,2048]{2,1,0:T(8,128)(2,1)}, u32[]{:S(2)}) copy-start(bf16[3,8,2048]{2,1,0:T(8,128)(2,1)} %param.10) | copy-start | bytes 294916
  0.7 500.3 %copy-start.15 = (s32[16]{0:T(128)S(1)}, s32[16]{0:T(128)}, u32[]{:S(2)}) copy-start(s32[16]{0:T(128)} %param.11) | copy-start | bytes 196
  3.9 471.8 %collective-permute-start = (bf16[2,256,2048]{2,1,0:T(8,128)(2,1)}, bf16[2,256,2048]{2,1,0:T(8,128)(2,1)}, u32[]{:S(2)}, u32[]{:S(2)}) collective-permute-start(bf16[2,256,2048]{2,1,0:T(8,128)(2,1)} %slice.25), channel_id=1, source_target_pairs={{0,8},{1,9},{2,10},{3,11},{4,12},{5,13},{6,14},{7,15},{16,24},{17,... | collective-permute-start | bytes 6291464 | tf_op jit(solution)/shard_map/ppermute | solution.py:16
  11.1 490.2 %collective-permute-start.1 = (bf16[2,256,2048]{2,1,0:T(8,128)(2,1)}, bf16[2,256,2048]{2,1,0:T(8,128)(2,1)}, u32[]{:S(2)}, u32[]{:S(2)}) collective-permute-start(bf16[2,256,2048]{2,1,0:T(8,128)(2,1)} %slice.25), channel_id=1, source_target_pairs={{0,7},{1,8},{2,9},{3,10},{4,11},{5,12},{6,13},{7,14},{8,15},{16,23... | collective-permute-start | bytes 6291464 | tf_op jit(solution)/shard_map/ppermute | solution.py:16
  16.1 503.7 %collective-permute-start.2 = (bf16[2,256,2048]{2,1,0:T(8,128)(2,1)}, bf16[2,256,2048]{2,1,0:T(8,128)(2,1)}, u32[]{:S(2)}, u32[]{:S(2)}) collective-permute-start(bf16[2,256,2048]{2,1,0:T(8,128)(2,1)} %slice.25), channel_id=1, source_target_pairs={{0,6},{1,7},{2,8},{3,9},{4,10},{5,11},{6,12},{7,13},{8,14},{9,15},... | collective-permute-start | bytes 6291464 | tf_op jit(solution)/shard_map/ppermute | solution.py:16
  19.9 11.4 %collective-permute-start.8 = (bf16[8,2048]{0,1:T(8,128)(2,1)S(1)}, bf16[8,2048]{0,1:T(8,128)(2,1)S(1)}, u32[]{:S(2)}, u32[]{:S(2)}) collective-permute-start(bf16[8,2048]{0,1:T(8,128)(2,1)S(1)} %bitcast.125), channel_id=1, source_target_pairs={{0,1},{1,2},{2,3},{3,4},{4,5},{5,6},{6,7},{7,8},{8,9},{9,10},{10,1... | collective-permute-start | bytes 98312 | tf_op jit(solution)/shard_map/ppermute | solution.py:102
  31.2 11.3 %collective-permute-start.9 = (bf16[8,2048]{0,1:T(8,128)(2,1)S(1)}, bf16[8,2048]{0,1:T(8,128)(2,1)S(1)}, u32[]{:S(2)}, u32[]{:S(2)}) collective-permute-start(bf16[8,2048]{0,1:T(8,128)(2,1)S(1)} %collective-permute-done.8), channel_id=1, source_target_pairs={{0,1},{1,2},{2,3},{3,4},{4,5},{5,6},{6,7},{7,8},{8,9},{9,10},{10,1... | collective-permute-start | bytes 98312 | tf_op jit(solution)/shard_map/ppermute | solution.py:102
  42.5 38.2 %collective-permute-start.10 = (bf16[8,2048]{0,1:T(8,128)(2,1)S(1)}, bf16[8,2048]{0,1:T(8,128)(2,1)S(1)}, u32[]{:S(2)}, u32[]{:S(2)}) collective-permute-start(bf16[8,2048]{0,1:T(8,128)(2,1)S(1)} %collective-permute-done.9), channel_id=1, source_target_pairs={{0,1},{1,2},{2,3},{3,4},{4,5},{5,6},{6,7},{7,8},{8,9},{9,10},{10,1... | collective-permute-start | bytes 98312 | tf_op jit(solution)/shard_map/ppermute | solution.py:102
  80.8 80.6 %collective-permute-start.11 = (bf16[8,2048]{0,1:T(8,128)(2,1)S(1)}, bf16[8,2048]{0,1:T(8,128)(2,1)S(1)}, u32[]{:S(2)}, u32[]{:S(2)}) collective-permute-start(bf16[8,2048]{0,1:T(8,128)(2,1)S(1)} %collective-permute-done.10), channel_id=1, source_target_pairs={{0,1},{1,2},{2,3},{3,4},{4,5},{5,6},{6,7},{7,8},{8,9},{9,10},{10,1... | collective-permute-start | bytes 98312 | tf_op jit(solution)/shard_map/ppermute | solution.py:102
  162.2 11.3 %collective-permute-start.12 = (bf16[8,2048]{0,1:T(8,128)(2,1)S(1)}, bf16[8,2048]{0,1:T(8,128)(2,1)S(1)}, u32[]{:S(2)}, u32[]{:S(2)}) collective-permute-start(bf16[8,2048]{0,1:T(8,128)(2,1)S(1)} %collective-permute-done.11), channel_id=1, source_target_pairs={{0,1},{1,2},{2,3},{3,4},{4,5},{5,6},{6,7},{7,8},{8,9},{9,10},{10,1... | collective-permute-start | bytes 98312 | tf_op jit(solution)/shard_map/ppermute | solution.py:102
  174.3 11.3 %collective-permute-start.13 = (bf16[8,2048]{0,1:T(8,128)(2,1)S(1)}, bf16[8,2048]{0,1:T(8,128)(2,1)S(1)}, u32[]{:S(2)}, u32[]{:S(2)}) collective-permute-start(bf16[8,2048]{0,1:T(8,128)(2,1)S(1)} %collective-permute-done.12), channel_id=1, source_target_pairs={{0,1},{1,2},{2,3},{3,4},{4,5},{5,6},{6,7},{7,8},{8,9},{9,10},{10,1... | collective-permute-start | bytes 98312 | tf_op jit(solution)/shard_map/ppermute | solution.py:102
  186.4 11.3 %collective-permute-start.14 = (bf16[8,2048]{0,1:T(8,128)(2,1)S(1)}, bf16[8,2048]{0,1:T(8,128)(2,1)S(1)}, u32[]{:S(2)}, u32[]{:S(2)}) collective-permute-start(bf16[8,2048]{0,1:T(8,128)(2,1)S(1)} %collective-permute-done.13), channel_id=1, source_target_pairs={{0,1},{1,2},{2,3},{3,4},{4,5},{5,6},{6,7},{7,8},{8,9},{9,10},{10,1... | collective-permute-start | bytes 98312 | tf_op jit(solution)/shard_map/ppermute | solution.py:102
  198.5 119.4 %collective-permute-start.15 = (bf16[8,2048]{0,1:T(8,128)(2,1)S(1)}, bf16[8,2048]{0,1:T(8,128)(2,1)S(1)}, u32[]{:S(2)}, u32[]{:S(2)}) collective-permute-start(bf16[8,2048]{0,1:T(8,128)(2,1)S(1)} %collective-permute-done.14), channel_id=1, source_target_pairs={{0,1},{1,2},{2,3},{3,4},{4,5},{5,6},{6,7},{7,8},{8,9},{9,10},{10,1... | collective-permute-start | bytes 98312 | tf_op jit(solution)/shard_map/ppermute | solution.py:102
  318.7 12.8 %collective-permute-start.16 = (bf16[8,2048]{0,1:T(8,128)(2,1)S(1)}, bf16[8,2048]{0,1:T(8,128)(2,1)S(1)}, u32[]{:S(2)}, u32[]{:S(2)}) collective-permute-start(bf16[8,2048]{0,1:T(8,128)(2,1)S(1)} %collective-permute-done.15), channel_id=1, source_target_pairs={{0,1},{1,2},{2,3},{3,4},{4,5},{5,6},{6,7},{7,8},{8,9},{9,10},{10,1... | collective-permute-start | bytes 98312 | tf_op jit(solution)/shard_map/ppermute | solution.py:102
  332.3 11.3 %collective-permute-start.17 = (bf16[8,2048]{0,1:T(8,128)(2,1)S(1)}, bf16[8,2048]{0,1:T(8,128)(2,1)S(1)}, u32[]{:S(2)}, u32[]{:S(2)}) collective-permute-start(bf16[8,2048]{0,1:T(8,128)(2,1)S(1)} %collective-permute-done.16), channel_id=1, source_target_pairs={{0,1},{1,2},{2,3},{3,4},{4,5},{5,6},{6,7},{7,8},{8,9},{9,10},{10,1... | collective-permute-start | bytes 98312 | tf_op jit(solution)/shard_map/ppermute | solution.py:102
  344.4 30.2 %collective-permute-start.18 = (bf16[8,2048]{0,1:T(8,128)(2,1)S(1)}, bf16[8,2048]{0,1:T(8,128)(2,1)S(1)}, u32[]{:S(2)}, u32[]{:S(2)}) collective-permute-start(bf16[8,2048]{0,1:T(8,128)(2,1)S(1)} %collective-permute-done.17), channel_id=1, source_target_pairs={{0,1},{1,2},{2,3},{3,4},{4,5},{5,6},{6,7},{7,8},{8,9},{9,10},{10,1... | collective-permute-start | bytes 98312 | tf_op jit(solution)/shard_map/ppermute | solution.py:102
  347.2 182.0 %collective-permute-start.3 = (bf16[2,256,2048]{2,1,0:T(8,128)(2,1)}, bf16[2,256,2048]{2,1,0:T(8,128)(2,1)}, u32[]{:S(2)}, u32[]{:S(2)}) collective-permute-start(bf16[2,256,2048]{2,1,0:T(8,128)(2,1)} %slice.25), channel_id=1, source_target_pairs={{0,5},{1,6},{2,7},{3,8},{4,9},{5,10},{6,11},{7,12},{8,13},{9,14},{... | collective-permute-start | bytes 6291464 | tf_op jit(solution)/shard_map/ppermute | solution.py:16
  375.3 11.3 %collective-permute-start.19 = (bf16[8,2048]{0,1:T(8,128)(2,1)S(1)}, bf16[8,2048]{0,1:T(8,128)(2,1)S(1)}, u32[]{:S(2)}, u32[]{:S(2)}) collective-permute-start(bf16[8,2048]{0,1:T(8,128)(2,1)S(1)} %collective-permute-done.18), channel_id=1, source_target_pairs={{0,1},{1,2},{2,3},{3,4},{4,5},{5,6},{6,7},{7,8},{8,9},{9,10},{10,1... | collective-permute-start | bytes 98312 | tf_op jit(solution)/shard_map/ppermute | solution.py:102
  387.4 11.3 %collective-permute-start.20 = (bf16[8,2048]{0,1:T(8,128)(2,1)S(1)}, bf16[8,2048]{0,1:T(8,128)(2,1)S(1)}, u32[]{:S(2)}, u32[]{:S(2)}) collective-permute-start(bf16[8,2048]{0,1:T(8,128)(2,1)S(1)} %collective-permute-done.19), channel_id=1, source_target_pairs={{0,1},{1,2},{2,3},{3,4},{4,5},{5,6},{6,7},{7,8},{8,9},{9,10},{10,1... | collective-permute-start | bytes 98312 | tf_op jit(solution)/shard_map/ppermute | solution.py:102
  399.5 11.3 %collective-permute-start.21 = (bf16[8,2048]{0,1:T(8,128)(2,1)S(1)}, bf16[8,2048]{0,1:T(8,128)(2,1)S(1)}, u32[]{:S(2)}, u32[]{:S(2)}) collective-permute-start(bf16[8,2048]{0,1:T(8,128)(2,1)S(1)} %collective-permute-done.20), channel_id=1, source_target_pairs={{0,1},{1,2},{2,3},{3,4},{4,5},{5,6},{6,7},{7,8},{8,9},{9,10},{10,1... | collective-permute-start | bytes 98312 | tf_op jit(solution)/shard_map/ppermute | solution.py:102
  410.8 93.1 %copy-start.12 = (bf16[8,2048]{0,1:T(8,128)(2,1)}, bf16[8,2048]{0,1:T(8,128)(2,1)S(1)}, u32[]{:S(2)}) copy-start(bf16[8,2048]{0,1:T(8,128)(2,1)S(1)} %collective-permute-done.21) | copy-start | bytes 98308
  410.8 35.5 %collective-permute-start.22 = (bf16[8,2048]{0,1:T(8,128)(2,1)S(1)}, bf16[8,2048]{0,1:T(8,128)(2,1)S(1)}, u32[]{:S(2)}, u32[]{:S(2)}) collective-permute-start(bf16[8,2048]{0,1:T(8,128)(2,1)S(1)} %collective-permute-done.21), channel_id=1, source_target_pairs={{0,1},{1,2},{2,3},{3,4},{4,5},{5,6},{6,7},{7,8},{8,9},{9,10},{10,1... | collective-permute-start | bytes 98312 | tf_op jit(solution)/shard_map/ppermute | solution.py:102
  446.4 57.6 %copy-start.13 = (bf16[8,2048]{0,1:T(8,128)(2,1)}, bf16[8,2048]{0,1:T(8,128)(2,1)S(1)}, u32[]{:S(2)}) copy-start(bf16[8,2048]{0,1:T(8,128)(2,1)S(1)} %collective-permute-done.22) | copy-start | bytes 98308
  446.4 84.6 %collective-permute-start.4 = (bf16[2,256,2048]{2,1,0:T(8,128)(2,1)}, bf16[2,256,2048]{2,1,0:T(8,128)(2,1)}, u32[]{:S(2)}, u32[]{:S(2)}) collective-permute-start(bf16[2,256,2048]{2,1,0:T(8,128)(2,1)} %slice.25), channel_id=1, source_target_pairs={{0,4},{1,5},{2,6},{3,7},{4,8},{5,9},{6,10},{7,11},{8,12},{9,13},{1... | collective-permute-start | bytes 6291464 | tf_op jit(solution)/shard_map/ppermute | solution.py:16
  475.7 66.7 %collective-permute-start.5 = (bf16[2,256,2048]{2,1,0:T(8,128)(2,1)}, bf16[2,256,2048]{2,1,0:T(8,128)(2,1)}, u32[]{:S(2)}, u32[]{:S(2)}) collective-permute-start(bf16[2,256,2048]{2,1,0:T(8,128)(2,1)} %slice.25), channel_id=1, source_target_pairs={{0,3},{1,4},{2,5},{3,6},{4,7},{5,8},{6,9},{7,10},{8,11},{9,12},{10... | collective-permute-start | bytes 6291464 | tf_op jit(solution)/shard_map/ppermute | solution.py:16
  501.4 86.0 %collective-permute-start.6 = (bf16[2,256,2048]{2,1,0:T(8,128)(2,1)}, bf16[2,256,2048]{2,1,0:T(8,128)(2,1)}, u32[]{:S(2)}, u32[]{:S(2)}) collective-permute-start(bf16[2,256,2048]{2,1,0:T(8,128)(2,1)} %slice.25), channel_id=1, source_target_pairs={{0,2},{1,3},{2,4},{3,5},{4,6},{5,7},{6,8},{7,9},{8,10},{9,11},{10,... | collective-permute-start | bytes 6291464 | tf_op jit(solution)/shard_map/ppermute | solution.py:16
  519.7 69.4 %collective-permute-start.7 = (bf16[2,256,2048]{2,1,0:T(8,128)(2,1)}, bf16[2,256,2048]{2,1,0:T(8,128)(2,1)S(1)}, u32[]{:S(2)}, u32[]{:S(2)}) collective-permute-start(bf16[2,256,2048]{2,1,0:T(8,128)(2,1)} %slice.25), channel_id=1, source_target_pairs={{0,1},{1,2},{2,3},{3,4},{4,5},{5,6},{6,7},{7,8},{8,9},{9,10},{10,1... | collective-permute-start | bytes 6291464 | tf_op jit(solution)/shard_map/ppermute | solution.py:16
  597.6 280.2 %copy-start.16 = (f32[2048]{0:T(1024)S(1)}, f32[2048]{0:T(1024)}, u32[]{:S(2)}) copy-start(f32[2048]{0:T(1024)} %param.9) | copy-start | bytes 24580
  882.5 67.4 %all-to-all-start.2 = ((bf16[16,8,16]{2,1,0:T(8,128)(2,1)}), bf16[16,8,16]{2,1,0:T(8,128)(2,1)S(1)}, u32[]{:S(2)}, u32[]{:S(2)}) async-start(bf16[16,8,16]{2,1,0:T(8,128)(2,1)} %bitcast.20), calls=%async_computation.2 | async-start | bytes 65536 | tf_op jit(solution)/shard_map/all_to_all | solution.py:152
  949.9 10.1 %all-to-all-start.1 = ((bf16[16,8,16]{2,1,0:T(8,128)(2,1)}), bf16[16,8,16]{2,1,0:T(8,128)(2,1)S(1)}, u32[]{:S(2)}, u32[]{:S(2)}) async-start(bf16[16,8,16]{2,1,0:T(8,128)(2,1)} %bitcast.6), calls=%async_computation.1 | async-start | bytes 65536 | tf_op jit(solution)/shard_map/all_to_all | solution.py:149
  960.0 17.8 %all-to-all-start = ((bf16[16,8,2048]{2,1,0:T(8,128)(2,1)}), bf16[16,8,2048]{2,1,0:T(8,128)(2,1)S(1)}, u32[]{:S(2)}, u32[]{:S(2)}) async-start(bf16[16,8,2048]{2,1,0:T(8,128)(2,1)} %convert_element_type.69), calls=%async_computation | async-start | bytes 1048576 | tf_op jit(solution)/shard_map/all_to_all | solution.py:146
  (13 other events, 22.9 us)
